TPU v7x, 32 devices: a whole 2x2x4 slice. The times are simulated.
32 devices in a mesh: section: 8 (over z, x), expert: 4 (over y, core).
Axes of the slice: x: 2, y: 2, z: 4, core: 2. Of those that a mesh axis runs over, the one named last changes fastest.
Arguments:
- entering: bfloat16 [2, 2, 128, 3584], P(None, None, 'expert'), may hold values from -6 to 6
- norm_gain: float32 [8, 3584], P('section'), may hold values from 0.5 to 1.5
- w_gate: bfloat16 [8, 3584, 2048], P('section', None, 'expert'), may hold values from -0.09375 to 0.09375
- w_up: bfloat16 [8, 3584, 2048], P('section', None, 'expert'), may hold values from -0.09375 to 0.09375
- w_down: bfloat16 [8, 2048, 3584], P('section', 'expert'), may hold values from -0.1875 to 0.1875
- route_ids: int32 [2, 2, 8, 128, 8], P(None, None, 'section', 'expert'), may hold values from 0 to 255, as said below
- route_scores: float32 [2, 2, 8, 128, 8], P(None, None, 'section', 'expert'), may hold values from 0.05 to 1
Outputs:
- leaving: bfloat16 [2, 2, 128, 3584], P(None, None, 'expert', 'section')
Inputs may be any that keep to these rules, and one draw needn't show every extreme that they name: `route_ids`: A token's 8 ids are distinct. In every block of 32 tokens (one direction, micro-batch and layer), at most 2 tokens name any one expert below 2, and in every such block exactly 2 tokens name one of them.
All inputs are finite; a program needn't handle non-finite values.
Results may differ from a plain program's by a relative error of at most 0.0072.
Values may be sent and summed in bfloat16 or wider, within the bound.
No kernel may reach another device: no remote copies, remote signals or barrier semaphores. Data moves between devices by JAX's collectives and lax.ppermute only.
A program may use at most 64 MiB of HBM per device.

v0:
```python
import jax
import jax.numpy as jnp
from jax import lax
from jax.sharding import PartitionSpec as P

GROUP = 2
CAP = 2


norm_eps = 1e-06
route_scale = 2.5


def from_behind(value, axis, steps):
    count = lax.axis_size(axis)
    initial, last = (max(0, -steps), min(count, count - steps))
    return lax.ppermute(value, axis, [(source, source + steps) for source in range(initial, last)])


def on_device(entering, norm_gain, w_gate, w_up, w_down, route_ids, route_scores):
    sections = lax.axis_size("section")
    spread = lax.axis_size("expert")
    section = lax.axis_index("section")
    window = spread // GROUP
    micro = entering.shape[1]
    tokens = entering.shape[2]
    width = entering.shape[3]
    gain = norm_gain[0]
    wgate = w_gate[0]
    wup = w_up[0]
    wdown = w_down[0]
    steps = micro + sections - 1
    earlier = (jnp.arange(tokens)[:, None] > jnp.arange(tokens)[None, :]).astype(jnp.float32)
    expert_iota = jnp.arange(window, dtype=jnp.int32)
    slot_iota = jnp.arange(CAP, dtype=jnp.float32)

    def prepare(x, ids, scores):
        xf = x.astype(jnp.float32)
        normed = (
            xf * lax.rsqrt(jnp.mean(xf * xf, axis=-1, keepdims=True) + norm_eps) * gain
        ).astype(jnp.bfloat16)
        weights = route_scale * scores / jnp.sum(scores, axis=-1, keepdims=True)
        hit = (ids[:, :, None] == expert_iota).astype(jnp.float32)
        count = jnp.sum(hit, axis=1)
        share = jnp.sum(weights[:, :, None] * hit, axis=1)
        before = jnp.dot(earlier, count, precision=lax.Precision.HIGHEST)
        place = count.T[:, None, :] * (before.T[:, None, :] == slot_iota[None, :, None]).astype(
            jnp.float32
        )
        blocks = jnp.einsum(
            "ect,td->ecd", place.astype(jnp.bfloat16), normed, preferred_element_type=jnp.float32
        ).astype(jnp.bfloat16)
        sending = jnp.repeat(blocks, GROUP, axis=0)
        comb = place * share.T[:, None, :]
        return (sending, comb)

    def expert_rows(received):
        count = received.shape[1]
        rows = received.reshape(-1, width)
        gate = jnp.dot(rows, wgate, preferred_element_type=jnp.float32)
        up = jnp.dot(rows, wup, preferred_element_type=jnp.float32)
        act = (jax.nn.silu(gate) * up).astype(jnp.bfloat16)
        part = (
            jnp.dot(act, wdown, preferred_element_type=jnp.float32)
            .astype(jnp.bfloat16)
            .reshape(spread, count, width)
        )
        back = lax.all_to_all(part, "expert", split_axis=0, concat_axis=0, tiled=True)
        return jnp.sum(back.astype(jnp.float32).reshape(window, GROUP, count, width), axis=1)

    def finish(x, comb, result):
        added = jnp.einsum("ect,ecd->td", comb, result, precision=lax.Precision.HIGHEST)
        return (x.astype(jnp.float32) + added).astype(jnp.bfloat16)

    def advance(step, carry):
        prev_f, prev_r, done_f, done_r = carry
        from_f = from_behind(prev_f, "section", 1)
        from_r = from_behind(prev_r, "section", -1)
        feed_index = jnp.clip(step, 0, micro - 1)
        feed_f = lax.dynamic_index_in_dim(entering[0], feed_index, 0, keepdims=False)
        feed_r = lax.dynamic_index_in_dim(entering[1], feed_index, 0, keepdims=False)
        x_f = jnp.where(section == 0, feed_f, from_f)
        x_r = jnp.where(section == sections - 1, feed_r, from_r)
        index_f = jnp.clip(step - section, 0, micro - 1)
        index_r = jnp.clip(step - (sections - 1 - section), 0, micro - 1)
        ids_f = lax.dynamic_index_in_dim(route_ids[0, :, 0], index_f, 0, keepdims=False)
        ids_r = lax.dynamic_index_in_dim(route_ids[1, :, 0], index_r, 0, keepdims=False)
        sc_f = lax.dynamic_index_in_dim(route_scores[0, :, 0], index_f, 0, keepdims=False)
        sc_r = lax.dynamic_index_in_dim(route_scores[1, :, 0], index_r, 0, keepdims=False)
        send_f, comb_f = prepare(x_f, ids_f, sc_f)
        send_r, comb_r = prepare(x_r, ids_r, sc_r)
        both = jnp.concatenate([send_f, send_r], axis=1)
        result = expert_rows(
            lax.all_to_all(both, "expert", split_axis=0, concat_axis=0, tiled=True)
        )
        result_f = result[:, :CAP]
        result_r = result[:, CAP:]
        out_f = finish(x_f, comb_f, result_f)
        out_r = finish(x_r, comb_r, result_r)
        leave_index = step - (sections - 1)
        safe_index = jnp.clip(leave_index, 0, micro - 1)
        valid = leave_index >= 0
        done_f = jnp.where(
            valid & (section == sections - 1),
            lax.dynamic_update_index_in_dim(done_f, out_f, safe_index, 0),
            done_f,
        )
        done_r = jnp.where(
            valid & (section == 0),
            lax.dynamic_update_index_in_dim(done_r, out_r, safe_index, 0),
            done_r,
        )
        return (out_f, out_r, done_f, done_r)

    blank = jnp.zeros((tokens, width), jnp.bfloat16)
    store = jnp.zeros((micro, tokens, width), jnp.bfloat16)
    unused_f, unused_r, done_f, done_r = lax.fori_loop(
        0, steps, advance, (blank, blank, store, store)
    )
    term_f = jnp.where(section == sections - 1, done_f.astype(jnp.float32), 0.0)
    term_r = jnp.where(section == 0, done_r.astype(jnp.float32), 0.0)
    final_f, final_r = (
        lax.psum_scatter(
            term_f.astype(jnp.bfloat16), "section", scatter_dimension=2, tiled=True
        ).astype(jnp.float32),
        lax.psum_scatter(
            term_r.astype(jnp.bfloat16), "section", scatter_dimension=2, tiled=True
        ).astype(jnp.float32),
    )
    return jnp.stack([final_f, final_r]).astype(jnp.bfloat16)


def solution(mesh):
    return jax.shard_map(
        on_device,
        mesh=mesh,
        in_specs=(
            P(None, None, "expert", None),
            P("section", None),
            P("section", None, "expert"),
            P("section", None, "expert"),
            P("section", "expert", None),
            P(None, None, "section", "expert", None),
            P(None, None, "section", "expert", None),
        ),
        out_specs=P(None, None, "expert", "section"),
        check_vma=False,
    )
```

profile of v0, /device:TPU:0, one launch (start us, length us, event | category | flops | bytes accessed | tf_op | source)
XLA Modules:
  0.0 506.9 jit_solution(1015763250389403229)
XLA Ops:
  6.6 354.7 %while.23 = (s32[]{:T(128)}, bf16[32,3584]{1,0:T(8,128)(2,1)S(1)}, bf16[32,3584]{1,0:T(8,128)(2,1)S(1)}, bf16[2,32,3584]{2,1,0:T(8,128)(2,1)S(1)}, bf16[2,32,358...) while((s32[]{:T(128)}, bf16[32,3584]{1,0:T(8,128)(2,1)S(1)}, ...), condition=%wide.region_10.11_spmd.clone.clone, body=%wide.region_0.10_spmd.clone.clone.sunk | while | flops 192499216 | bytes 21841904 | solution.py:117
  6.7 4.9 collective-permute-start.1
  16.7 3.8 collective-permute-done
  22.2 7.0 %all_to_all.30 = bf16[4,4,3584]{2,1,0:T(4,128)(2,1)S(1)} all-to-all(bf16[4,4,3584]{2,1,0:T(4,128)(2,1)S(1)} %pad_maximum_fusion.3), channel_id=1, replica_groups=mesh['section'=8,'expert'=4] {'expert'}, dimensions={0} | all-to-all | bytes 229376 | tf_op jit(solution)/shard_map/while/body/eval_jaxpr/all_to_all | solution.py:94
  31.9 4.3 convolution_convert_fusion.8
  40.2 4.4 all-to-all-done.1
  46.1 4.4 collective-permute-start.1
  55.7 4.4 collective-permute-done
  61.2 6.8 %all_to_all.30 = bf16[4,4,3584]{2,1,0:T(4,128)(2,1)S(1)} all-to-all(bf16[4,4,3584]{2,1,0:T(4,128)(2,1)S(1)} %pad_maximum_fusion.3), channel_id=1, replica_groups=mesh['section'=8,'expert'=4] {'expert'}, dimensions={0} | all-to-all | bytes 229376 | tf_op jit(solution)/shard_map/while/body/eval_jaxpr/all_to_all | solution.py:94
  70.6 4.3 convolution_convert_fusion.8
  79.0 4.4 all-to-all-done.1
  84.8 4.6 collective-permute-start.1
  94.6 5.0 collective-permute-done
  100.7 6.8 %all_to_all.30 = bf16[4,4,3584]{2,1,0:T(4,128)(2,1)S(1)} all-to-all(bf16[4,4,3584]{2,1,0:T(4,128)(2,1)S(1)} %pad_maximum_fusion.3), channel_id=1, replica_groups=mesh['section'=8,'expert'=4] {'expert'}, dimensions={0} | all-to-all | bytes 229376 | tf_op jit(solution)/shard_map/while/body/eval_jaxpr/all_to_all | solution.py:94
  110.1 4.3 convolution_convert_fusion.8
  118.5 4.4 all-to-all-done.1
  124.3 4.6 collective-permute-start.1
  134.1 5.0 collective-permute-done
  140.2 6.8 %all_to_all.30 = bf16[4,4,3584]{2,1,0:T(4,128)(2,1)S(1)} all-to-all(bf16[4,4,3584]{2,1,0:T(4,128)(2,1)S(1)} %pad_maximum_fusion.3), channel_id=1, replica_groups=mesh['section'=8,'expert'=4] {'expert'}, dimensions={0} | all-to-all | bytes 229376 | tf_op jit(solution)/shard_map/while/body/eval_jaxpr/all_to_all | solution.py:94
  149.6 4.3 convolution_convert_fusion.8
  158.0 4.4 all-to-all-done.1
  163.8 4.6 collective-permute-start.1
  173.6 5.0 collective-permute-done
  179.7 6.8 %all_to_all.30 = bf16[4,4,3584]{2,1,0:T(4,128)(2,1)S(1)} all-to-all(bf16[4,4,3584]{2,1,0:T(4,128)(2,1)S(1)} %pad_maximum_fusion.3), channel_id=1, replica_groups=mesh['section'=8,'expert'=4] {'expert'}, dimensions={0} | all-to-all | bytes 229376 | tf_op jit(solution)/shard_map/while/body/eval_jaxpr/all_to_all | solution.py:94
  189.1 4.3 convolution_convert_fusion.8
  197.5 4.4 all-to-all-done.1
  203.3 4.6 collective-permute-start.1
  213.1 5.0 collective-permute-done
  219.2 6.8 %all_to_all.30 = bf16[4,4,3584]{2,1,0:T(4,128)(2,1)S(1)} all-to-all(bf16[4,4,3584]{2,1,0:T(4,128)(2,1)S(1)} %pad_maximum_fusion.3), channel_id=1, replica_groups=mesh['section'=8,'expert'=4] {'expert'}, dimensions={0} | all-to-all | bytes 229376 | tf_op jit(solution)/shard_map/while/body/eval_jaxpr/all_to_all | solution.py:94
  228.6 4.3 convolution_convert_fusion.8
  237.0 4.4 all-to-all-done.1
  242.8 4.6 collective-permute-start.1
  252.6 5.0 collective-permute-done
  258.7 6.8 %all_to_all.30 = bf16[4,4,3584]{2,1,0:T(4,128)(2,1)S(1)} all-to-all(bf16[4,4,3584]{2,1,0:T(4,128)(2,1)S(1)} %pad_maximum_fusion.3), channel_id=1, replica_groups=mesh['section'=8,'expert'=4] {'expert'}, dimensions={0} | all-to-all | bytes 229376 | tf_op jit(solution)/shard_map/while/body/eval_jaxpr/all_to_all | solution.py:94
  268.2 4.3 convolution_convert_fusion.8
  276.5 4.4 all-to-all-done.1
  282.3 4.6 collective-permute-start.1
  292.1 5.0 collective-permute-done
  298.2 6.8 %all_to_all.30 = bf16[4,4,3584]{2,1,0:T(4,128)(2,1)S(1)} all-to-all(bf16[4,4,3584]{2,1,0:T(4,128)(2,1)S(1)} %pad_maximum_fusion.3), channel_id=1, replica_groups=mesh['section'=8,'expert'=4] {'expert'}, dimensions={0} | all-to-all | bytes 229376 | tf_op jit(solution)/shard_map/while/body/eval_jaxpr/all_to_all | solution.py:94
  307.7 4.3 convolution_convert_fusion.8
  316.0 4.4 all-to-all-done.1
  321.8 4.6 collective-permute-start.1
  331.6 5.0 collective-permute-done
  337.7 6.8 %all_to_all.30 = bf16[4,4,3584]{2,1,0:T(4,128)(2,1)S(1)} all-to-all(bf16[4,4,3584]{2,1,0:T(4,128)(2,1)S(1)} %pad_maximum_fusion.3), channel_id=1, replica_groups=mesh['section'=8,'expert'=4] {'expert'}, dimensions={0} | all-to-all | bytes 229376 | tf_op jit(solution)/shard_map/while/body/eval_jaxpr/all_to_all | solution.py:94
  347.2 4.3 convolution_convert_fusion.8
  355.5 4.4 all-to-all-done.1
  369.8 62.4 %reduce-scatter.9.cloned.1.call-done = bf16[448,64]{1,0:T(8,128)(2,1)} async-done(((bf16[3584,64]{1,0:T(8,128)(2,1)}), bf16[448,64]{1,0:T(8,128)(2,1)}) %reduce-scatter.9.cloned.1.call-update) | async-done | bytes 57360
  433.3 64.9 %reduce-scatter.7.cloned.1.call-done = bf16[448,64]{1,0:T(8,128)(2,1)} async-done(((bf16[3584,64]{1,0:T(8,128)(2,1)}), bf16[448,64]{1,0:T(8,128)(2,1)}) %reduce-scatter.7.cloned.1.call-update) | async-done | bytes 57360
  (333 shorter events, 140.6 us)
Async XLA Ops:
  6.5 425.6 %reduce-scatter.9.cloned.1.call-start = ((), (), s32[]{:S(2)}) async-start(), calls=%async_computation.5 | async-start | bytes 1032192
  6.7 14.6 %collective-permute-start.1 = (bf16[32,3584]{1,0:T(8,128)(2,1)S(1)}, bf16[32,3584]{1,0:T(8,128)(2,1)S(1)}, u32[]{:S(2)}, u32[]{:S(2)}) collective-permute-start(bf16[32,3584]{1,0:T(8,128)(2,1)S(1)} %broadcast_select_fusion.5), channel_id=1, source_target_pairs={{0,4},{4,8},{8,12},{12,16},{16,20},{20,24},{24,28},{1,5},{5,9},{9,... | collective-permute-start | bytes 688136 | tf_op jit(solution)/shard_map/while/body/eval_jaxpr/ppermute | solution.py:17
  11.6 9.0 %collective-permute-start = (bf16[32,3584]{1,0:T(8,128)(2,1)S(1)}, bf16[32,3584]{1,0:T(8,128)(2,1)S(1)}, u32[]{:S(2)}, u32[]{:S(2)}) collective-permute-start(bf16[32,3584]{1,0:T(8,128)(2,1)S(1)} %broadcast_select_fusion.4), channel_id=1, source_target_pairs={{4,0},{8,4},{12,8},{16,12},{20,16},{24,20},{28,24},{5,1},{9,5},{13... | collective-permute-start | bytes 688136 | tf_op jit(solution)/shard_map/while/body/eval_jaxpr/ppermute | solution.py:17
  36.9 7.7 %all-to-all-start.1 = ((bf16[4,4,3584]{2,1,0:T(4,128)(2,1)}), bf16[4,4,3584]{2,1,0:T(4,128)(2,1)S(1)}, u32[]{:S(2)}, u32[]{:S(2)}) async-start(bf16[4,4,3584]{2,1,0:T(4,128)(2,1)} %reshape.181), calls=%async_computation.1 | async-start | bytes 229376 | tf_op jit(solution)/shard_map/while/body/eval_jaxpr/all_to_all | solution.py:68
  46.1 14.2 %collective-permute-start.1 = (bf16[32,3584]{1,0:T(8,128)(2,1)S(1)}, bf16[32,3584]{1,0:T(8,128)(2,1)S(1)}, u32[]{:S(2)}, u32[]{:S(2)}) collective-permute-start(bf16[32,3584]{1,0:T(8,128)(2,1)S(1)} %broadcast_select_fusion.5), channel_id=1, source_target_pairs={{0,4},{4,8},{8,12},{12,16},{16,20},{20,24},{24,28},{1,5},{5,9},{9,... | collective-permute-start | bytes 688136 | tf_op jit(solution)/shard_map/while/body/eval_jaxpr/ppermute | solution.py:17
  50.5 9.6 %collective-permute-start = (bf16[32,3584]{1,0:T(8,128)(2,1)S(1)}, bf16[32,3584]{1,0:T(8,128)(2,1)S(1)}, u32[]{:S(2)}, u32[]{:S(2)}) collective-permute-start(bf16[32,3584]{1,0:T(8,128)(2,1)S(1)} %broadcast_select_fusion.4), channel_id=1, source_target_pairs={{4,0},{8,4},{12,8},{16,12},{20,16},{24,20},{28,24},{5,1},{9,5},{13... | collective-permute-start | bytes 688136 | tf_op jit(solution)/shard_map/while/body/eval_jaxpr/ppermute | solution.py:17
  75.6 7.7 %all-to-all-start.1 = ((bf16[4,4,3584]{2,1,0:T(4,128)(2,1)}), bf16[4,4,3584]{2,1,0:T(4,128)(2,1)S(1)}, u32[]{:S(2)}, u32[]{:S(2)}) async-start(bf16[4,4,3584]{2,1,0:T(4,128)(2,1)} %reshape.181), calls=%async_computation.1 | async-start | bytes 229376 | tf_op jit(solution)/shard_map/while/body/eval_jaxpr/all_to_all | solution.py:68
  84.8 14.9 %collective-permute-start.1 = (bf16[32,3584]{1,0:T(8,128)(2,1)S(1)}, bf16[32,3584]{1,0:T(8,128)(2,1)S(1)}, u32[]{:S(2)}, u32[]{:S(2)}) collective-permute-start(bf16[32,3584]{1,0:T(8,128)(2,1)S(1)} %broadcast_select_fusion.5), channel_id=1, source_target_pairs={{0,4},{4,8},{8,12},{12,16},{16,20},{20,24},{24,28},{1,5},{5,9},{9,... | collective-permute-start | bytes 688136 | tf_op jit(solution)/shard_map/while/body/eval_jaxpr/ppermute | solution.py:17
  89.4 10.1 %collective-permute-start = (bf16[32,3584]{1,0:T(8,128)(2,1)S(1)}, bf16[32,3584]{1,0:T(8,128)(2,1)S(1)}, u32[]{:S(2)}, u32[]{:S(2)}) collective-permute-start(bf16[32,3584]{1,0:T(8,128)(2,1)S(1)} %broadcast_select_fusion.4), channel_id=1, source_target_pairs={{4,0},{8,4},{12,8},{16,12},{20,16},{24,20},{28,24},{5,1},{9,5},{13... | collective-permute-start | bytes 688136 | tf_op jit(solution)/shard_map/while/body/eval_jaxpr/ppermute | solution.py:17
  115.1 7.7 %all-to-all-start.1 = ((bf16[4,4,3584]{2,1,0:T(4,128)(2,1)}), bf16[4,4,3584]{2,1,0:T(4,128)(2,1)S(1)}, u32[]{:S(2)}, u32[]{:S(2)}) async-start(bf16[4,4,3584]{2,1,0:T(4,128)(2,1)} %reshape.181), calls=%async_computation.1 | async-start | bytes 229376 | tf_op jit(solution)/shard_map/while/body/eval_jaxpr/all_to_all | solution.py:68
  124.3 14.9 %collective-permute-start.1 = (bf16[32,3584]{1,0:T(8,128)(2,1)S(1)}, bf16[32,3584]{1,0:T(8,128)(2,1)S(1)}, u32[]{:S(2)}, u32[]{:S(2)}) collective-permute-start(bf16[32,3584]{1,0:T(8,128)(2,1)S(1)} %broadcast_select_fusion.5), channel_id=1, source_target_pairs={{0,4},{4,8},{8,12},{12,16},{16,20},{20,24},{24,28},{1,5},{5,9},{9,... | collective-permute-start | bytes 688136 | tf_op jit(solution)/shard_map/while/body/eval_jaxpr/ppermute | solution.py:17
  128.9 10.1 %collective-permute-start = (bf16[32,3584]{1,0:T(8,128)(2,1)S(1)}, bf16[32,3584]{1,0:T(8,128)(2,1)S(1)}, u32[]{:S(2)}, u32[]{:S(2)}) collective-permute-start(bf16[32,3584]{1,0:T(8,128)(2,1)S(1)} %broadcast_select_fusion.4), channel_id=1, source_target_pairs={{4,0},{8,4},{12,8},{16,12},{20,16},{24,20},{28,24},{5,1},{9,5},{13... | collective-permute-start | bytes 688136 | tf_op jit(solution)/shard_map/while/body/eval_jaxpr/ppermute | solution.py:17
  154.6 7.7 %all-to-all-start.1 = ((bf16[4,4,3584]{2,1,0:T(4,128)(2,1)}), bf16[4,4,3584]{2,1,0:T(4,128)(2,1)S(1)}, u32[]{:S(2)}, u32[]{:S(2)}) async-start(bf16[4,4,3584]{2,1,0:T(4,128)(2,1)} %reshape.181), calls=%async_computation.1 | async-start | bytes 229376 | tf_op jit(solution)/shard_map/while/body/eval_jaxpr/all_to_all | solution.py:68
  163.8 14.9 %collective-permute-start.1 = (bf16[32,3584]{1,0:T(8,128)(2,1)S(1)}, bf16[32,3584]{1,0:T(8,128)(2,1)S(1)}, u32[]{:S(2)}, u32[]{:S(2)}) collective-permute-start(bf16[32,3584]{1,0:T(8,128)(2,1)S(1)} %broadcast_select_fusion.5), channel_id=1, source_target_pairs={{0,4},{4,8},{8,12},{12,16},{16,20},{20,24},{24,28},{1,5},{5,9},{9,... | collective-permute-start | bytes 688136 | tf_op jit(solution)/shard_map/while/body/eval_jaxpr/ppermute | solution.py:17
  168.4 10.1 %collective-permute-start = (bf16[32,3584]{1,0:T(8,128)(2,1)S(1)}, bf16[32,3584]{1,0:T(8,128)(2,1)S(1)}, u32[]{:S(2)}, u32[]{:S(2)}) collective-permute-start(bf16[32,3584]{1,0:T(8,128)(2,1)S(1)} %broadcast_select_fusion.4), channel_id=1, source_target_pairs={{4,0},{8,4},{12,8},{16,12},{20,16},{24,20},{28,24},{5,1},{9,5},{13... | collective-permute-start | bytes 688136 | tf_op jit(solution)/shard_map/while/body/eval_jaxpr/ppermute | solution.py:17
  194.1 7.7 %all-to-all-start.1 = ((bf16[4,4,3584]{2,1,0:T(4,128)(2,1)}), bf16[4,4,3584]{2,1,0:T(4,128)(2,1)S(1)}, u32[]{:S(2)}, u32[]{:S(2)}) async-start(bf16[4,4,3584]{2,1,0:T(4,128)(2,1)} %reshape.181), calls=%async_computation.1 | async-start | bytes 229376 | tf_op jit(solution)/shard_map/while/body/eval_jaxpr/all_to_all | solution.py:68
  203.3 14.9 %collective-permute-start.1 = (bf16[32,3584]{1,0:T(8,128)(2,1)S(1)}, bf16[32,3584]{1,0:T(8,128)(2,1)S(1)}, u32[]{:S(2)}, u32[]{:S(2)}) collective-permute-start(bf16[32,3584]{1,0:T(8,128)(2,1)S(1)} %broadcast_select_fusion.5), channel_id=1, source_target_pairs={{0,4},{4,8},{8,12},{12,16},{16,20},{20,24},{24,28},{1,5},{5,9},{9,... | collective-permute-start | bytes 688136 | tf_op jit(solution)/shard_map/while/body/eval_jaxpr/ppermute | solution.py:17
  207.9 10.1 %collective-permute-start = (bf16[32,3584]{1,0:T(8,128)(2,1)S(1)}, bf16[32,3584]{1,0:T(8,128)(2,1)S(1)}, u32[]{:S(2)}, u32[]{:S(2)}) collective-permute-start(bf16[32,3584]{1,0:T(8,128)(2,1)S(1)} %broadcast_select_fusion.4), channel_id=1, source_target_pairs={{4,0},{8,4},{12,8},{16,12},{20,16},{24,20},{28,24},{5,1},{9,5},{13... | collective-permute-start | bytes 688136 | tf_op jit(solution)/shard_map/while/body/eval_jaxpr/ppermute | solution.py:17
  233.6 7.7 %all-to-all-start.1 = ((bf16[4,4,3584]{2,1,0:T(4,128)(2,1)}), bf16[4,4,3584]{2,1,0:T(4,128)(2,1)S(1)}, u32[]{:S(2)}, u32[]{:S(2)}) async-start(bf16[4,4,3584]{2,1,0:T(4,128)(2,1)} %reshape.181), calls=%async_computation.1 | async-start | bytes 229376 | tf_op jit(solution)/shard_map/while/body/eval_jaxpr/all_to_all | solution.py:68
  242.8 14.9 %collective-permute-start.1 = (bf16[32,3584]{1,0:T(8,128)(2,1)S(1)}, bf16[32,3584]{1,0:T(8,128)(2,1)S(1)}, u32[]{:S(2)}, u32[]{:S(2)}) collective-permute-start(bf16[32,3584]{1,0:T(8,128)(2,1)S(1)} %broadcast_select_fusion.5), channel_id=1, source_target_pairs={{0,4},{4,8},{8,12},{12,16},{16,20},{20,24},{24,28},{1,5},{5,9},{9,... | collective-permute-start | bytes 688136 | tf_op jit(solution)/shard_map/while/body/eval_jaxpr/ppermute | solution.py:17
  247.4 10.1 %collective-permute-start = (bf16[32,3584]{1,0:T(8,128)(2,1)S(1)}, bf16[32,3584]{1,0:T(8,128)(2,1)S(1)}, u32[]{:S(2)}, u32[]{:S(2)}) collective-permute-start(bf16[32,3584]{1,0:T(8,128)(2,1)S(1)} %broadcast_select_fusion.4), channel_id=1, source_target_pairs={{4,0},{8,4},{12,8},{16,12},{20,16},{24,20},{28,24},{5,1},{9,5},{13... | collective-permute-start | bytes 688136 | tf_op jit(solution)/shard_map/while/body/eval_jaxpr/ppermute | solution.py:17
  273.2 7.7 %all-to-all-start.1 = ((bf16[4,4,3584]{2,1,0:T(4,128)(2,1)}), bf16[4,4,3584]{2,1,0:T(4,128)(2,1)S(1)}, u32[]{:S(2)}, u32[]{:S(2)}) async-start(bf16[4,4,3584]{2,1,0:T(4,128)(2,1)} %reshape.181), calls=%async_computation.1 | async-start | bytes 229376 | tf_op jit(solution)/shard_map/while/body/eval_jaxpr/all_to_all | solution.py:68
  282.3 14.9 %collective-permute-start.1 = (bf16[32,3584]{1,0:T(8,128)(2,1)S(1)}, bf16[32,3584]{1,0:T(8,128)(2,1)S(1)}, u32[]{:S(2)}, u32[]{:S(2)}) collective-permute-start(bf16[32,3584]{1,0:T(8,128)(2,1)S(1)} %broadcast_select_fusion.5), channel_id=1, source_target_pairs={{0,4},{4,8},{8,12},{12,16},{16,20},{20,24},{24,28},{1,5},{5,9},{9,... | collective-permute-start | bytes 688136 | tf_op jit(solution)/shard_map/while/body/eval_jaxpr/ppermute | solution.py:17
  286.9 10.1 %collective-permute-start = (bf16[32,3584]{1,0:T(8,128)(2,1)S(1)}, bf16[32,3584]{1,0:T(8,128)(2,1)S(1)}, u32[]{:S(2)}, u32[]{:S(2)}) collective-permute-start(bf16[32,3584]{1,0:T(8,128)(2,1)S(1)} %broadcast_select_fusion.4), channel_id=1, source_target_pairs={{4,0},{8,4},{12,8},{16,12},{20,16},{24,20},{28,24},{5,1},{9,5},{13... | collective-permute-start | bytes 688136 | tf_op jit(solution)/shard_map/while/body/eval_jaxpr/ppermute | solution.py:17
  312.7 7.7 %all-to-all-start.1 = ((bf16[4,4,3584]{2,1,0:T(4,128)(2,1)}), bf16[4,4,3584]{2,1,0:T(4,128)(2,1)S(1)}, u32[]{:S(2)}, u32[]{:S(2)}) async-start(bf16[4,4,3584]{2,1,0:T(4,128)(2,1)} %reshape.181), calls=%async_computation.1 | async-start | bytes 229376 | tf_op jit(solution)/shard_map/while/body/eval_jaxpr/all_to_all | solution.py:68
  321.8 14.9 %collective-permute-start.1 = (bf16[32,3584]{1,0:T(8,128)(2,1)S(1)}, bf16[32,3584]{1,0:T(8,128)(2,1)S(1)}, u32[]{:S(2)}, u32[]{:S(2)}) collective-permute-start(bf16[32,3584]{1,0:T(8,128)(2,1)S(1)} %broadcast_select_fusion.5), channel_id=1, source_target_pairs={{0,4},{4,8},{8,12},{12,16},{16,20},{20,24},{24,28},{1,5},{5,9},{9,... | collective-permute-start | bytes 688136 | tf_op jit(solution)/shard_map/while/body/eval_jaxpr/ppermute | solution.py:17
  326.4 10.1 %collective-permute-start = (bf16[32,3584]{1,0:T(8,128)(2,1)S(1)}, bf16[32,3584]{1,0:T(8,128)(2,1)S(1)}, u32[]{:S(2)}, u32[]{:S(2)}) collective-permute-start(bf16[32,3584]{1,0:T(8,128)(2,1)S(1)} %broadcast_select_fusion.4), channel_id=1, source_target_pairs={{4,0},{8,4},{12,8},{16,12},{20,16},{24,20},{28,24},{5,1},{9,5},{13... | collective-permute-start | bytes 688136 | tf_op jit(solution)/shard_map/while/body/eval_jaxpr/ppermute | solution.py:17
  352.2 7.7 %all-to-all-start.1 = ((bf16[4,4,3584]{2,1,0:T(4,128)(2,1)}), bf16[4,4,3584]{2,1,0:T(4,128)(2,1)S(1)}, u32[]{:S(2)}, u32[]{:S(2)}) async-start(bf16[4,4,3584]{2,1,0:T(4,128)(2,1)} %reshape.181), calls=%async_computation.1 | async-start | bytes 229376 | tf_op jit(solution)/shard_map/while/body/eval_jaxpr/all_to_all | solution.py:68
  365.6 132.6 %reduce-scatter.7.cloned.1.call-start = ((), (), s32[]{:S(2)}) async-start(), calls=%async_computation.4 | async-start | bytes 1032192
Sparse Core Ops, SparseCore 0:
  365.7 66.4 reduce-scatter.8
  435.5 62.6 reduce-scatter.6
where the time goes:
time: 511 us; the launch traced here: 507 us
  waiting for transfers between devices  210 us (41%)
  starting transfers between devices  82.7 us (16%)
  matrix products  80.7 us (16%)
  blocking collectives  61.5 us (12%)
  local copies, waits for them, and re-layouts  42.2 us (8%)
  other arithmetic  14.4 us (3%)
  between operations  13.5 us (3%)
    unnamed x4, waiting for transfers between devices  127 us
    all_to_all x9, blocking collectives, advance(): lax.all_to_all(both, 'expert', split_axis=0, concat_axis=0, tiled=True)  61.5 us
    ppermute x18, starting transfers between devices, from_behind(): lax.ppermute(value, axis, [(source, source + steps) for source in range(i...  52.8 us
    ppermute x18, waiting for transfers between devices, from_behind(): lax.ppermute(value, axis, [(source, source + steps) for source in range(i...  43.6 us
    all_to_all x9, waiting for transfers between devices, expert_rows(): lax.all_to_all(part, 'expert', split_axis=0, concat_axis=0, tiled=True)  39.4 us
    dot_general x9, matrix products, expert_rows(): jnp.dot(act, wdown, preferred_element_type=jnp.float32).astype(jnp.bfloat16)  38.8 us
    all_to_all x9, starting transfers between devices, expert_rows(): lax.all_to_all(part, 'expert', split_axis=0, concat_axis=0, tiled=True)  29.8 us
    dot_general x9, matrix products, expert_rows(): gate = jnp.dot(rows, wgate, preferred_element_type=jnp.float32)  23.5 us
  transfers between devices with their start and end apart: 29, of which 21 were waited for; matrix products, arithmetic and copies ran while one was open for 8% of the time, Pallas kernels for 0%

commit v1 on v0

v1 whole, which is shorter than its diff:
```python
import functools

import jax
import jax.numpy as jnp
from jax import lax
from jax.experimental import pallas as pl
from jax.experimental.pallas import tpu as pltpu
from jax.sharding import PartitionSpec as P

GROUP = 2
CAP = 2

norm_eps = 1e-06
route_scale = 2.5

F32 = jnp.float32
BF16 = jnp.bfloat16
LANES = 128
AXES = ("section", "expert")

VMEM = pltpu.VMEM
SMEM = pltpu.SMEM


def iota(shape, dim):
    return lax.broadcasted_iota(jnp.int32, shape, dim)


def mm(a, b):
    return jnp.dot(a, b, preferred_element_type=F32)


def route_kernel(me_ref, ids_ref, scores_ref, x_ref, *refs, tokens, window, slots):
    spread = len(refs) - 1
    outs, rows_ref = refs[:spread], refs[spread]
    count, width = x_ref.shape
    ids = ids_ref[...]
    scores = scores_ref[...]
    weights = route_scale * scores / jnp.sum(scores, axis=-1, keepdims=True)
    place_i = iota((count, count), 0)
    place_j = iota((count, count), 1)
    block_of = lambda v: jnp.floor((v.astype(F32) + 0.5) * (1.0 / tokens))
    earlier = ((place_j < place_i) & (block_of(place_i) == block_of(place_j))).astype(BF16)
    lane = iota((count, LANES), 1)
    token_lane = iota((slots, count), 1).astype(F32)
    base = block_of(iota((count, 1), 0)) * CAP
    hits, shares = [], []
    stacked = jnp.zeros((count, LANES), F32)
    for e in range(window):
        same = ids == e
        hit = jnp.sum(jnp.where(same, 1.0, 0.0), axis=-1, keepdims=True)
        hits.append(hit)
        shares.append(jnp.sum(jnp.where(same, weights, 0.0), axis=-1, keepdims=True))
        stacked = jnp.where(lane == e, hit, stacked)
    before = mm(earlier, stacked.astype(BF16))
    x = x_ref[...]
    meta_lane = iota((slots, LANES), 1)
    for e in range(window):
        slot = (base + before[:, e:e + 1]).astype(jnp.int32)
        taken = jnp.where(lane == slot, hits[e], 0.0)
        pick = taken.T[:slots]
        token = jnp.sum(pick * token_lane + pick, axis=-1, keepdims=True) - 1.0
        w = jnp.sum((taken * shares[e]).T[:slots], axis=-1, keepdims=True)
        high = w.astype(BF16).astype(F32)
        mid = (w - high).astype(BF16).astype(F32)
        low = w - high - mid
        meta = jnp.where(meta_lane == 0, token, 0.0)
        meta = jnp.where(meta_lane == 1, high, meta)
        meta = jnp.where(meta_lane == 2, mid, meta)
        meta = jnp.where(meta_lane == 3, low, meta)
        rows_ref[e, :, :width] = mm(pick.astype(BF16), x).astype(BF16)
        rows_ref[e, :, width:] = meta.astype(BF16)
    me = me_ref[0]
    for k in range(spread):
        peer = lax.rem(me + k, spread)
        outs[k][...] = rows_ref[lax.div(peer, GROUP)]


def feed_forward(h, wg_ref, wu_ref, wd_ref):
    gate = mm(h, wg_ref[...])
    up = mm(h, wu_ref[...])
    act = (gate / (1.0 + jnp.exp(-gate)) * up).astype(BF16)
    return mm(act, wd_ref[...])


def first_kernel(me_ref, gain_ref, wg_ref, wu_ref, wd_ref, *refs, sections, feats):
    spread = len(refs) - 1
    ins, out_ref = refs[:spread], refs[spread]
    width = gain_ref.shape[1]
    slots = ins[0].shape[0]
    room = out_ref.shape[2] - feats
    x = jnp.concatenate([r[:, :width].astype(F32) for r in ins], axis=0)
    mean = jnp.mean(x * x, axis=-1, keepdims=True)
    h = (x * lax.rsqrt(mean + norm_eps) * gain_ref[...]).astype(BF16)
    part = feed_forward(h, wg_ref, wu_ref, wd_ref).astype(BF16)
    me = me_ref[0]
    for k in range(spread):
        block = lax.rem(me - k + spread, spread)
        meta = ins[k][:, width:width + room]
        for s in range(sections):
            out_ref[s * spread + block, :, :feats] = part[k * slots:(k + 1) * slots, s * feats:(s + 1) * feats]
            out_ref[s * spread + block, :, feats:] = meta


def round_kernel(gain_ref, wg_ref, wu_ref, wd_ref, in_ref, out_ref, last_ref, *, sections, feats):
    count, slots, padded = in_ref.shape
    spread = count // sections
    rows = spread * slots
    width = sections * feats
    pieces = []
    total = jnp.zeros((rows, 1), F32)
    for s in range(sections):
        piece = in_ref[s * spread:(s + 1) * spread, :, :].astype(F32).reshape(rows, padded)[:, :feats]
        total = total + jnp.sum(piece * piece, axis=-1, keepdims=True)
        pieces.append(piece)
    scale = lax.rsqrt(total * (1.0 / width) + norm_eps)
    gate = jnp.zeros((rows, wg_ref.shape[1]), F32)
    up = jnp.zeros((rows, wg_ref.shape[1]), F32)
    for s in range(sections):
        h = (pieces[s] * scale * gain_ref[s:s + 1, :]).astype(BF16)
        gate = gate + mm(h, wg_ref[s * feats:(s + 1) * feats, :])
        up = up + mm(h, wu_ref[s * feats:(s + 1) * feats, :])
    act = (gate / (1.0 + jnp.exp(-gate)) * up).astype(BF16)
    part = mm(act, wd_ref[...]).astype(BF16)
    for s in range(sections):
        piece = part[:, s * feats:(s + 1) * feats]
        for b in range(spread):
            out_ref[s * spread + b, :, :feats] = piece[b * slots:(b + 1) * slots]
            out_ref[s * spread + b, :, feats:] = jnp.zeros((slots, padded - feats), BF16)
    depth = in_ref[:spread, :, :].astype(F32).reshape(rows, padded)[:, feats:feats + 1]
    last_ref[0] = jnp.max(depth).astype(jnp.int32)


def apply_parts(step, parts, x, cols, rows_tab, feats):
    tokens, padded = x.shape
    count = parts.shape[0]
    chosen = (iota((tokens, count), 0).astype(F32) == rows_tab[0:1, :]) & (rows_tab[4:5, :] == step)
    added = jnp.zeros((tokens, padded), F32)
    for n in (1, 2, 3):
        added = added + mm(jnp.where(chosen, rows_tab[n:n + 1, :], 0.0).astype(BF16), parts)
    lane = iota((tokens, padded), 1)
    x = jnp.where(lane < feats, x.astype(F32) + added, 0.0).astype(BF16)
    pick = (iota((count, tokens), 1).astype(F32) == cols[:, 0:1]).astype(BF16)
    send = jnp.where(iota((count, padded), 1) == feats, cols[:, 5:6], mm(pick, x))
    return x, send.astype(BF16)


def table_kernel(x_ref, in_ref, x_out, send_out, cols_out, rows_out, *, sections, feats):
    count, slots, padded = in_ref.shape
    tokens = x_ref.shape[0]
    total = count * slots
    per = total // sections
    parts = in_ref[...].reshape(total, padded)
    meta = parts[:, feats:feats + 4].astype(F32)
    token = meta[:, 0:1]
    pick = (iota((total, tokens), 1).astype(F32) == token).astype(F32)
    hit = [jnp.minimum(jnp.sum(pick[l * per:(l + 1) * per], axis=0, keepdims=True), 1.0) for l in range(sections)]
    ahead, behind = [None] * sections, [None] * sections
    run_a = run_b = jnp.zeros((1, tokens), F32)
    for l in range(sections):
        ahead[l] = run_a
        run_a = run_a + hit[l]
        m = sections - 1 - l
        behind[m] = run_b
        run_b = run_b + hit[m]
    forward = iota((1, tokens), 1) < tokens // 2
    level = [
        jnp.sum(pick[l * per:(l + 1) * per] * jnp.where(forward, ahead[l], behind[l]), axis=-1, keepdims=True)
        for l in range(sections)
    ]
    level = jnp.concatenate(level, axis=0)
    depth = jnp.max(run_a)
    lane = iota((total, LANES), 1)
    cols = jnp.where(lane == 0, token, 0.0)
    for n in (1, 2, 3):
        cols = jnp.where(lane == n, meta[:, n:n + 1], cols)
    cols = jnp.where(lane == 4, level, cols)
    cols = jnp.where(lane == 5, depth, cols)
    rows_tab = cols.T[:8]
    cols_out[...] = cols
    rows_out[...] = rows_tab
    x, send = apply_parts(0.0, parts, x_ref[...], cols, rows_tab, feats)
    x_out[...] = x
    send_out[...] = send.reshape(count, slots, padded)


def update_kernel(step_ref, x_ref, in_ref, cols_ref, rows_ref, x_out, send_out, *, feats):
    count, slots, padded = in_ref.shape
    step = step_ref[0].astype(F32)
    parts = in_ref[...].reshape(count * slots, padded)
    x, send = apply_parts(step, parts, x_ref[...], cols_ref[...], rows_ref[...], feats)
    x_out[...] = x
    send_out[...] = send.reshape(count, slots, padded)


def call(kernel, out_shape, in_spaces, out_spaces, name, scratch=(), limit=None):
    spec = lambda space: pl.BlockSpec(memory_space=space)
    single = not isinstance(out_shape, (list, tuple))
    return pl.pallas_call(
        kernel,
        out_shape=out_shape,
        in_specs=[spec(s) for s in in_spaces],
        out_specs=spec(out_spaces[0]) if single else [spec(s) for s in out_spaces],
        scratch_shapes=list(scratch),
        compiler_params=pltpu.CompilerParams(vmem_limit_bytes=limit),
        name=name,
    )


def on_device(entering, norm_gain, w_gate, w_up, w_down, route_ids, route_scores):
    sections = lax.axis_size("section")
    spread = lax.axis_size("expert")
    section = lax.axis_index("section")
    peer = lax.axis_index("expert")
    window = spread // GROUP
    ways, micro, tokens, width = entering.shape
    everyone = ways * micro * tokens
    slots = ways * micro * CAP
    feats = width // sections
    padded = (feats // LANES + 1) * LANES
    devices = sections * spread
    topk = route_ids.shape[-1]

    wg, wu, wd = (w_gate[0], w_up[0], w_down[0])
    me = peer.astype(jnp.int32).reshape(1)
    flat = entering.reshape(everyone, width)
    sds = jax.ShapeDtypeStruct

    rows = call(
        functools.partial(route_kernel, tokens=tokens, window=window, slots=slots),
        [sds((slots, width + LANES), BF16)] * spread,
        [SMEM, VMEM, VMEM, VMEM],
        [VMEM] * spread,
        "route",
        scratch=[VMEM((window, slots, width + LANES), BF16)],
    )(me, route_ids.reshape(everyone, topk), route_scores.reshape(everyone, topk), flat)
    received = [rows[0]] + [
        lax.ppermute(rows[k], "expert", [(y, (y + k) % spread) for y in range(spread)]) for k in range(1, spread)
    ]
    message = sds((devices, slots, padded), BF16)
    swap = lambda v: lax.all_to_all(v, AXES, split_axis=0, concat_axis=0, tiled=True)
    parts = call(
        functools.partial(first_kernel, sections=sections, feats=feats),
        message,
        [SMEM] + [VMEM] * (4 + spread),
        [VMEM],
        "first",
    )(me, norm_gain, wg, wu, wd, *received)
    own = lax.dynamic_slice(flat, (0, section * feats), (everyone, feats))
    own = jnp.pad(own, ((0, 0), (0, padded - feats)))
    x, send, cols, rows_tab = call(
        functools.partial(table_kernel, sections=sections, feats=feats),
        [sds((everyone, padded), BF16), message, sds((devices * slots, LANES), F32), sds((8, devices * slots), F32)],
        [VMEM, VMEM],
        [VMEM] * 4,
        "table",
    )(own, swap(parts))
    gain = norm_gain.reshape(sections, feats)

    def more(carry):
        return carry[0] < carry[1]

    def turn(carry):
        step, unused, x, send = carry
        parts, last = call(
            functools.partial(round_kernel, sections=sections, feats=feats),
            [message, sds((1,), jnp.int32)],
            [VMEM] * 5,
            [VMEM, SMEM],
            "round",
        )(gain, wg, wu, wd, swap(send))
        x, send = call(
            functools.partial(update_kernel, feats=feats),
            [sds((everyone, padded), BF16), message],
            [SMEM] + [VMEM] * 4,
            [VMEM] * 2,
            "update",
        )(step.reshape(1), x, swap(parts), cols, rows_tab)
        return (step + 1, last[0], x, send)

    carry = (jnp.int32(1), jnp.int32(2), x, send)
    x = lax.while_loop(more, turn, carry)[2]
    return x[:, :feats].reshape(ways, micro, tokens, feats)


def solution(mesh):
    return jax.shard_map(
        on_device,
        mesh=mesh,
        in_specs=(
            P(None, None, "expert", None),
            P("section", None),
            P("section", None, "expert"),
            P("section", None, "expert"),
            P("section", "expert", None),
            P(None, None, "section", "expert", None),
            P(None, None, "section", "expert", None),
        ),
        out_specs=P(None, None, "expert", "section"),
        check_vma=False,
    )
```

time: 511 us -> 149 us (0.29)
  waiting for transfers between devices: 210 us -> 40.6 us
  matrix products: 80.7 us -> 0 us
  starting transfers between devices: 82.7 us -> 18.3 us
  Pallas kernels: 0 us -> 37.8 us
  local copies, waits for them, and re-layouts: 42.2 us -> 10.6 us
  blocking collectives: 61.5 us -> 38.9 us
  other arithmetic: 14.4 us -> 0.04 us
  between operations: 13.5 us -> 0.07 us
    unnamed x4 -> x0, waiting for transfers between devices: 127 us -> none
    dot_general x72 -> x0, matrix products: 80.7 us -> none  [the longest x9 38.8 us: expert_rows(): jnp.dot(act, wdown, preferred_element_type=jnp.float32).astype(jnp.bfloat16)]
    ppermute x18 -> x3, starting transfers between devices: 52.8 us -> 4.46 us  [on_device(): lax.ppermute(rows[k], 'expert', [(y, (y + k) % spread) for y in range(spr...]
    ppermute x18 -> x3, waiting for transfers between devices: 43.6 us -> 2.16 us  [on_device(): lax.ppermute(rows[k], 'expert', [(y, (y + k) % spread) for y in range(spr...]
    pallas_call x0 -> x9, Pallas kernels: none -> 37.8 us  [the longest x3 21.5 us: turn(): call(functools.partial(round_kernel, sections=sections, feats=feats), [me...]
    slice x36 -> x0, local copies, waits for them, and re-layouts: 24.5 us -> none  [the longest x9 11.1 us: advance(): entering[1]]
    all_to_all x9 -> x3, blocking collectives: 61.5 us -> 38.9 us  [on_device(): lax.all_to_all(v, AXES, split_axis=0, concat_axis=0, tiled=True)]
    all_to_all x9 -> x4, starting transfers between devices: 29.8 us -> 13.8 us  [on_device(): lax.all_to_all(v, AXES, split_axis=0, concat_axis=0, tiled=True)]
  transfers between devices with their start and end apart: 29 -> 7, of which waited for: 21 -> 7; matrix products, arithmetic and copies ran while one was open for 8% -> 3% of each run, Pallas kernels for 0% -> 0%
where the time goes in v1:
time: 149 us; the launch traced here: 148 us
  waiting for transfers between devices  40.6 us (27%)
  blocking collectives  38.9 us (26%)
  Pallas kernels  37.8 us (25%)
  starting transfers between devices  18.3 us (12%)
  local copies, waits for them, and re-layouts  10.6 us (7%)
  loops' own time  2.04 us (1%)
    all_to_all x3, blocking collectives, on_device(): lax.all_to_all(v, AXES, split_axis=0, concat_axis=0, tiled=True)  38.9 us
    all_to_all x4, waiting for transfers between devices, on_device(): lax.all_to_all(v, AXES, split_axis=0, concat_axis=0, tiled=True)  38.5 us
    pallas_call x3, Pallas kernels, turn(): call(functools.partial(round_kernel, sections=sections, feats=feats), [me...  21.5 us
    all_to_all x4, starting transfers between devices, on_device(): lax.all_to_all(v, AXES, split_axis=0, concat_axis=0, tiled=True)  13.8 us
    pallas_call x1, Pallas kernels, on_device(): call(functools.partial(first_kernel, sections=sections, feats=feats), mes...  7.18 us
    unnamed x14, local copies, waits for them, and re-layouts  4.81 us
    pallas_call x3, Pallas kernels, turn(): call(functools.partial(update_kernel, feats=feats), [sds((everyone, padde...  4.47 us
    ppermute x3, starting transfers between devices, on_device(): lax.ppermute(rows[k], 'expert', [(y, (y + k) % spread) for y in range(spr...  4.46 us
  transfers between devices with their start and end apart: 7, of which 7 were waited for; matrix products, arithmetic and copies ran while one was open for 3% of the time, Pallas kernels for 0%

profile of v1, /device:TPU:0, one launch (start us, length us, event | category | flops | bytes accessed | tf_op | source)
XLA Modules:
  0.0 148.3 jit_solution(803887726246691497)
XLA Ops:
  0.0 1.4 copy.8
  1.4 1.4 copy.9
  2.9 2.7 %route.1 = (bf16[8,3712]{1,0:T(8,128)(2,1)}, bf16[8,3712]{1,0:T(8,128)(2,1)}, bf16[8,3712]{1,0:T(8,128)(2,1)}, bf16[8,3712]{1,0:T(8,128)(2,1)}) custom-call(s32[1]{0:T(128)} %bitcast.3.me_ref, s32[128,8]{1,0:T(8,128)} %bitcast.24, f32[128,8]{1,0:T(8,128)} %bitcast.25, bf16[128,3584]{1,0:T(8,128)(2,1)} %bitcast.22), custom_call_target="tpu_custom_call" | custom-call | tf_op jit(solution)/shard_map/route/pallas_call | solution.py:229
  5.5 0.5 collective-permute-start
  6.0 2.5 %collective-permute-start.1 = (bf16[8,3712]{1,0:T(8,128)(2,1)}, bf16[8,3712]{1,0:T(8,128)(2,1)S(1)}, u32[]{:S(2)}, u32[]{:S(2)}) collective-permute-start(bf16[8,3712]{1,0:T(8,128)(2,1)} %get-tuple-element.71), channel_id=1, source_target_pairs={{0,2},{1,3},{2,0},{3,1},{4,6},{5,7},{6,4},{7,5},{8,10},{9,11},{10,... | collective-permute-start | bytes 178184 | tf_op jit(solution)/shard_map/ppermute | solution.py:238
  8.5 1.5 collective-permute-start.2
  10.0 0.1 collective-permute-done.refs_1_
  10.0 0.0 copy-start.3
  10.0 1.1 collective-permute-done.1.refs_2_
  11.2 0.0 copy-start.4
  11.2 1.0 collective-permute-done.2.refs_3_
  12.1 0.0 copy-start.5
  12.1 0.0 copy-done.3
  12.1 0.0 copy-done.4
  12.1 0.6 copy-done.5
  12.8 7.2 %first.1 = bf16[32,8,512]{2,1,0:T(8,128)(2,1)} custom-call(s32[1]{0:T(128)} %bitcast.3.me_ref, f32[1,3584]{1,0:T(1,128)} %gain_ref.1, bf16[3584,512]{1,0:T(8,128)(2,1)} %bitcast.15, bf16[3584,512]{1,0:T(8,128)(2,1)} %bitcast.17, bf16[512,3584]{1,0:T(8,128)(2,1)} %bitcast.19, bf16[8,3712]{1,0:T(8,128)(2,1)} %get-tuple-element.69.refs_0_, ...), custom_call_target="tpu_custom_call" | custom-call | tf_op jit(solution)/shard_map/first/pallas_call | solution.py:242
  19.9 6.0 %all-to-all-start.2 = ((bf16[32,8,512]{2,1,0:T(8,128)(2,1)}), bf16[32,8,512]{2,1,0:T(8,128)(2,1)S(1)}, u32[]{:S(2)}, u32[]{:S(2)}) async-start(bf16[32,8,512]{2,1,0:T(8,128)(2,1)} %first.1), calls=%async_computation.2 | async-start | bytes 524288 | tf_op jit(solution)/shard_map/all_to_all | solution.py:241
  25.9 0.0 copy-done.6
  26.0 0.1 reshape.25
  26.1 1.0 constant_dynamic-slice_fusion
  27.1 0.7 pad.4.x_ref
  27.8 8.7 %all-to-all-done.2.in_ref = bf16[32,8,512]{2,1,0:T(8,128)(2,1)S(1)} async-done(((bf16[32,8,512]{2,1,0:T(8,128)(2,1)}), bf16[32,8,512]{2,1,0:T(8,128)(2,1)S(1)}, u32[]{:S(2)}, u32[]{:S(2)}) %all-to-all-start.2) | async-done | bytes 262176 | tf_op jit(solution)/shard_map/all_to_all | solution.py:241
  36.5 0.7 copy-done.2
  37.2 1.9 %table.1 = (bf16[128,512]{1,0:T(8,128)(2,1)S(1)}, bf16[32,8,512]{2,1,0:T(8,128)(2,1)S(1)}, f32[256,128]{1,0:T(8,128)S(1)}, f32[8,256]{1,0:T(8,128)S(1)}) custom-call(bf16[128,512]{1,0:T(8,128)(2,1)} %pad.4.x_ref, bf16[32,8,512]{2,1,0:T(8,128)(2,1)} %copy-done.2), custom_call_target="tpu_custom_call" | custom-call | tf_op jit(solution)/shard_map/table/pallas_call | solution.py:251
  39.1 108.5 %while.14 = (s32[]{:T(128)}, s32[]{:T(128)}, bf16[128,512]{1,0:T(8,128)(2,1)S(1)}, bf16[32,8,512]{2,1,0:T(8,128)(2,1)S(1)}, f32[8,448]{1,0:T(8,128)S(1)}, /*inde...) while((s32[]{:T(128)}, s32[]{:T(128)}, ...), condition=%wide.region_1.2_spmd, body=%wide.region_0.1_spmd.sunk | while | flops 2 | bytes 2621617 | solution.py:282
  39.2 13.0 %all_to_all.17.in_ref = bf16[32,8,512]{2,1,0:T(8,128)(2,1)} all-to-all(bf16[32,8,512]{2,1,0:T(8,128)(2,1)S(1)} %get-tuple-element.180), channel_id=1, replica_groups=mesh['section'=8,'expert'=4] {'section','expert'}, dimensions={0} | all-to-all | bytes 524288 | tf_op jit(solution)/shard_map/while/body/all_to_all | solution.py:241
  52.1 7.2 %round.1 = (bf16[32,8,512]{2,1,0:T(8,128)(2,1)}, s32[1]{0:T(128)}) custom-call(f32[8,448]{1,0:T(8,128)S(1)} %get-tuple-element.192.gain_ref, bf16[3584,512]{1,0:T(8,128)(2,1)} %get-tuple-element.193.wg_ref, bf16[3584,512]{1,0:T(8,128)(2,1)} %get-tuple-element.194.wu_ref, bf16[512,3584]{1,0:T(8,128)(2,1)} %get-tuple-element.195.wd_ref, ...), custom_call_target="tpu_custom_call" | custom-call | tf_op jit(solution)/shard_map/while/body/round/pallas_call | solution.py:265
  59.3 2.6 %all-to-all-start.1 = ((bf16[32,8,512]{2,1,0:T(8,128)(2,1)}), bf16[32,8,512]{2,1,0:T(8,128)(2,1)S(1)}, u32[]{:S(2)}, u32[]{:S(2)}) async-start(bf16[32,8,512]{2,1,0:T(8,128)(2,1)} %get-tuple-element.163), calls=%async_computation.1 | async-start | bytes 524288 | tf_op jit(solution)/shard_map/while/body/all_to_all | solution.py:241
  61.9 0.7 copy.25.x_ref
  62.6 9.9 %all-to-all-done.1.in_ref = bf16[32,8,512]{2,1,0:T(8,128)(2,1)S(1)} async-done(((bf16[32,8,512]{2,1,0:T(8,128)(2,1)}), bf16[32,8,512]{2,1,0:T(8,128)(2,1)S(1)}, u32[]{:S(2)}, u32[]{:S(2)}) %all-to-all-start.1) | async-done | bytes 262176 | tf_op jit(solution)/shard_map/while/body/all_to_all | solution.py:241
  72.5 0.7 copy-done
  73.2 1.5 %update.1 = (bf16[128,512]{1,0:T(8,128)(2,1)S(1)}, bf16[32,8,512]{2,1,0:T(8,128)(2,1)S(1)}) custom-call(s32[1]{0:T(128)} %bitcast.14.step_ref, bf16[128,512]{1,0:T(8,128)(2,1)} %copy.25.x_ref, bf16[32,8,512]{2,1,0:T(8,128)(2,1)} %copy-done, f32[256,128]{1,0:T(8,128)S(1)} %get-tuple-element.196.cols_ref, f32[8,256]{1,0:T(8,128)S(1)} %get-tuple-element.197.rows_ref), custom_call_target="tpu_custom_call" | custom-call | tf_op jit(solution)/shard_map/while/body/update/pallas_call | solution.py:272
  75.3 13.0 %all_to_all.17.in_ref = bf16[32,8,512]{2,1,0:T(8,128)(2,1)} all-to-all(bf16[32,8,512]{2,1,0:T(8,128)(2,1)S(1)} %get-tuple-element.180), channel_id=1, replica_groups=mesh['section'=8,'expert'=4] {'section','expert'}, dimensions={0} | all-to-all | bytes 524288 | tf_op jit(solution)/shard_map/while/body/all_to_all | solution.py:241
  88.3 7.2 %round.1 = (bf16[32,8,512]{2,1,0:T(8,128)(2,1)}, s32[1]{0:T(128)}) custom-call(f32[8,448]{1,0:T(8,128)S(1)} %get-tuple-element.192.gain_ref, bf16[3584,512]{1,0:T(8,128)(2,1)} %get-tuple-element.193.wg_ref, bf16[3584,512]{1,0:T(8,128)(2,1)} %get-tuple-element.194.wu_ref, bf16[512,3584]{1,0:T(8,128)(2,1)} %get-tuple-element.195.wd_ref, ...), custom_call_target="tpu_custom_call" | custom-call | tf_op jit(solution)/shard_map/while/body/round/pallas_call | solution.py:265
  95.5 2.6 %all-to-all-start.1 = ((bf16[32,8,512]{2,1,0:T(8,128)(2,1)}), bf16[32,8,512]{2,1,0:T(8,128)(2,1)S(1)}, u32[]{:S(2)}, u32[]{:S(2)}) async-start(bf16[32,8,512]{2,1,0:T(8,128)(2,1)} %get-tuple-element.163), calls=%async_computation.1 | async-start | bytes 524288 | tf_op jit(solution)/shard_map/while/body/all_to_all | solution.py:241
  98.1 0.7 copy.25.x_ref
  98.7 9.9 %all-to-all-done.1.in_ref = bf16[32,8,512]{2,1,0:T(8,128)(2,1)S(1)} async-done(((bf16[32,8,512]{2,1,0:T(8,128)(2,1)}), bf16[32,8,512]{2,1,0:T(8,128)(2,1)S(1)}, u32[]{:S(2)}, u32[]{:S(2)}) %all-to-all-start.1) | async-done | bytes 262176 | tf_op jit(solution)/shard_map/while/body/all_to_all | solution.py:241
  108.7 0.7 copy-done
  109.4 1.5 %update.1 = (bf16[128,512]{1,0:T(8,128)(2,1)S(1)}, bf16[32,8,512]{2,1,0:T(8,128)(2,1)S(1)}) custom-call(s32[1]{0:T(128)} %bitcast.14.step_ref, bf16[128,512]{1,0:T(8,128)(2,1)} %copy.25.x_ref, bf16[32,8,512]{2,1,0:T(8,128)(2,1)} %copy-done, f32[256,128]{1,0:T(8,128)S(1)} %get-tuple-element.196.cols_ref, f32[8,256]{1,0:T(8,128)S(1)} %get-tuple-element.197.rows_ref), custom_call_target="tpu_custom_call" | custom-call | tf_op jit(solution)/shard_map/while/body/update/pallas_call | solution.py:272
  111.5 13.0 %all_to_all.17.in_ref = bf16[32,8,512]{2,1,0:T(8,128)(2,1)} all-to-all(bf16[32,8,512]{2,1,0:T(8,128)(2,1)S(1)} %get-tuple-element.180), channel_id=1, replica_groups=mesh['section'=8,'expert'=4] {'section','expert'}, dimensions={0} | all-to-all | bytes 524288 | tf_op jit(solution)/shard_map/while/body/all_to_all | solution.py:241
  124.5 7.2 %round.1 = (bf16[32,8,512]{2,1,0:T(8,128)(2,1)}, s32[1]{0:T(128)}) custom-call(f32[8,448]{1,0:T(8,128)S(1)} %get-tuple-element.192.gain_ref, bf16[3584,512]{1,0:T(8,128)(2,1)} %get-tuple-element.193.wg_ref, bf16[3584,512]{1,0:T(8,128)(2,1)} %get-tuple-element.194.wu_ref, bf16[512,3584]{1,0:T(8,128)(2,1)} %get-tuple-element.195.wd_ref, ...), custom_call_target="tpu_custom_call" | custom-call | tf_op jit(solution)/shard_map/while/body/round/pallas_call | solution.py:265
  131.7 2.6 %all-to-all-start.1 = ((bf16[32,8,512]{2,1,0:T(8,128)(2,1)}), bf16[32,8,512]{2,1,0:T(8,128)(2,1)S(1)}, u32[]{:S(2)}, u32[]{:S(2)}) async-start(bf16[32,8,512]{2,1,0:T(8,128)(2,1)} %get-tuple-element.163), calls=%async_computation.1 | async-start | bytes 524288 | tf_op jit(solution)/shard_map/while/body/all_to_all | solution.py:241
  134.3 0.7 copy.25.x_ref
  134.9 9.9 %all-to-all-done.1.in_ref = bf16[32,8,512]{2,1,0:T(8,128)(2,1)S(1)} async-done(((bf16[32,8,512]{2,1,0:T(8,128)(2,1)}), bf16[32,8,512]{2,1,0:T(8,128)(2,1)S(1)}, u32[]{:S(2)}, u32[]{:S(2)}) %all-to-all-start.1) | async-done | bytes 262176 | tf_op jit(solution)/shard_map/while/body/all_to_all | solution.py:241
  144.8 0.7 copy-done
  145.5 1.5 %update.1 = (bf16[128,512]{1,0:T(8,128)(2,1)S(1)}, bf16[32,8,512]{2,1,0:T(8,128)(2,1)S(1)}) custom-call(s32[1]{0:T(128)} %bitcast.14.step_ref, bf16[128,512]{1,0:T(8,128)(2,1)} %copy.25.x_ref, bf16[32,8,512]{2,1,0:T(8,128)(2,1)} %copy-done, f32[256,128]{1,0:T(8,128)S(1)} %get-tuple-element.196.cols_ref, f32[8,256]{1,0:T(8,128)S(1)} %get-tuple-element.197.rows_ref), custom_call_target="tpu_custom_call" | custom-call | tf_op jit(solution)/shard_map/while/body/update/pallas_call | solution.py:272
  147.7 0.0 copy-start.1
  147.7 0.6 copy-done.1
  (6 shorter events, 0.0 us)
Async XLA Ops:
  5.5 4.5 %collective-permute-start = (bf16[8,3712]{1,0:T(8,128)(2,1)}, bf16[8,3712]{1,0:T(8,128)(2,1)S(1)}, u32[]{:S(2)}, u32[]{:S(2)}) collective-permute-start(bf16[8,3712]{1,0:T(8,128)(2,1)} %get-tuple-element.70), channel_id=1, source_target_pairs={{0,1},{1,2},{2,3},{3,0},{4,5},{5,6},{6,7},{7,4},{8,9},{9,10},{10,1... | collective-permute-start | bytes 178184 | tf_op jit(solution)/shard_map/ppermute | solution.py:238
  6.0 5.2 %collective-permute-start.1 = (bf16[8,3712]{1,0:T(8,128)(2,1)}, bf16[8,3712]{1,0:T(8,128)(2,1)S(1)}, u32[]{:S(2)}, u32[]{:S(2)}) collective-permute-start(bf16[8,3712]{1,0:T(8,128)(2,1)} %get-tuple-element.71), channel_id=1, source_target_pairs={{0,2},{1,3},{2,0},{3,1},{4,6},{5,7},{6,4},{7,5},{8,10},{9,11},{10,... | collective-permute-start | bytes 178184 | tf_op jit(solution)/shard_map/ppermute | solution.py:238
  8.5 3.6 %collective-permute-start.2 = (bf16[8,3712]{1,0:T(8,128)(2,1)}, bf16[8,3712]{1,0:T(8,128)(2,1)S(1)}, u32[]{:S(2)}, u32[]{:S(2)}) collective-permute-start(bf16[8,3712]{1,0:T(8,128)(2,1)} %get-tuple-element.72), channel_id=1, source_target_pairs={{0,3},{1,0},{2,1},{3,2},{4,7},{5,4},{6,5},{7,6},{8,11},{9,8},{10,9... | collective-permute-start | bytes 178184 | tf_op jit(solution)/shard_map/ppermute | solution.py:238
  10.0 2.1 %copy-start.3 = (bf16[8,3712]{1,0:T(8,128)(2,1)}, bf16[8,3712]{1,0:T(8,128)(2,1)S(1)}, u32[]{:S(2)}) copy-start(bf16[8,3712]{1,0:T(8,128)(2,1)S(1)} %collective-permute-done.refs_1_) | copy-start | bytes 178180
  11.2 1.0 copy-start.4
  12.1 0.6 copy-start.5
  12.8 13.2 %copy-start.6 = (f32[1,3584]{1,0:T(1,128)S(1)}, f32[1,3584]{1,0:T(1,128)}, u32[]{:S(2)}) copy-start(f32[1,3584]{1,0:T(1,128)} %gain_ref.1) | copy-start | bytes 43012
  19.9 16.6 %all-to-all-start.2 = ((bf16[32,8,512]{2,1,0:T(8,128)(2,1)}), bf16[32,8,512]{2,1,0:T(8,128)(2,1)S(1)}, u32[]{:S(2)}, u32[]{:S(2)}) async-start(bf16[32,8,512]{2,1,0:T(8,128)(2,1)} %first.1), calls=%async_computation.2 | async-start | bytes 524288 | tf_op jit(solution)/shard_map/all_to_all | solution.py:241
  36.5 0.7 copy-start.2
  59.3 13.2 %all-to-all-start.1 = ((bf16[32,8,512]{2,1,0:T(8,128)(2,1)}), bf16[32,8,512]{2,1,0:T(8,128)(2,1)S(1)}, u32[]{:S(2)}, u32[]{:S(2)}) async-start(bf16[32,8,512]{2,1,0:T(8,128)(2,1)} %get-tuple-element.163), calls=%async_computation.1 | async-start | bytes 524288 | tf_op jit(solution)/shard_map/while/body/all_to_all | solution.py:241
  72.5 0.7 copy-start
  95.5 13.2 %all-to-all-start.1 = ((bf16[32,8,512]{2,1,0:T(8,128)(2,1)}), bf16[32,8,512]{2,1,0:T(8,128)(2,1)S(1)}, u32[]{:S(2)}, u32[]{:S(2)}) async-start(bf16[32,8,512]{2,1,0:T(8,128)(2,1)} %get-tuple-element.163), calls=%async_computation.1 | async-start | bytes 524288 | tf_op jit(solution)/shard_map/while/body/all_to_all | solution.py:241
  108.7 0.7 copy-start
  131.7 13.2 %all-to-all-start.1 = ((bf16[32,8,512]{2,1,0:T(8,128)(2,1)}), bf16[32,8,512]{2,1,0:T(8,128)(2,1)S(1)}, u32[]{:S(2)}, u32[]{:S(2)}) async-start(bf16[32,8,512]{2,1,0:T(8,128)(2,1)} %get-tuple-element.163), calls=%async_computation.1 | async-start | bytes 524288 | tf_op jit(solution)/shard_map/while/body/all_to_all | solution.py:241
  144.8 0.7 copy-start
  147.7 0.7 copy-start.1

commit v2 on v1

--- a/solution.py
+++ b/solution.py
@@ -30,37 +30,32 @@
     return jnp.dot(a, b, preferred_element_type=F32)
 
 
-def route_kernel(me_ref, ids_ref, scores_ref, x_ref, *refs, tokens, window, slots):
+def route_kernel(me_ref, ids_ref, scores_ref, x_ref, *refs, window, slots):
     spread = len(refs) - 1
     outs, rows_ref = refs[:spread], refs[spread]
+    groups, topk, tokens = ids_ref.shape
     count, width = x_ref.shape
-    ids = ids_ref[...]
-    scores = scores_ref[...]
-    weights = route_scale * scores / jnp.sum(scores, axis=-1, keepdims=True)
+    across = lambda ref: jnp.concatenate([ref[g] for g in range(groups)], axis=1)
+    ids = across(ids_ref)
+    scores = across(scores_ref)
+    weights = route_scale * scores / jnp.sum(scores, axis=0, keepdims=True)
+    block_of = lambda v: jnp.floor((v.astype(F32) + 0.5) * (1.0 / tokens))
     place_i = iota((count, count), 0)
     place_j = iota((count, count), 1)
-    block_of = lambda v: jnp.floor((v.astype(F32) + 0.5) * (1.0 / tokens))
-    earlier = ((place_j < place_i) & (block_of(place_i) == block_of(place_j))).astype(BF16)
-    lane = iota((count, LANES), 1)
+    earlier = ((place_i < place_j) & (block_of(place_i) == block_of(place_j))).astype(BF16)
     token_lane = iota((slots, count), 1).astype(F32)
-    base = block_of(iota((count, 1), 0)) * CAP
-    hits, shares = [], []
-    stacked = jnp.zeros((count, LANES), F32)
-    for e in range(window):
-        same = ids == e
-        hit = jnp.sum(jnp.where(same, 1.0, 0.0), axis=-1, keepdims=True)
-        hits.append(hit)
-        shares.append(jnp.sum(jnp.where(same, weights, 0.0), axis=-1, keepdims=True))
-        stacked = jnp.where(lane == e, hit, stacked)
-    before = mm(earlier, stacked.astype(BF16))
+    slot_row = iota((slots, count), 0).astype(F32)
+    base = block_of(iota((1, count), 1)) * CAP
+    same = [ids == e for e in range(window)]
+    hits = jnp.concatenate([jnp.sum(jnp.where(m, 1.0, 0.0), axis=0, keepdims=True) for m in same], axis=0)
+    before = mm(hits.astype(BF16), earlier)
     x = x_ref[...]
     meta_lane = iota((slots, LANES), 1)
     for e in range(window):
-        slot = (base + before[:, e:e + 1]).astype(jnp.int32)
-        taken = jnp.where(lane == slot, hits[e], 0.0)
-        pick = taken.T[:slots]
+        share = jnp.sum(jnp.where(same[e], weights, 0.0), axis=0, keepdims=True)
+        pick = jnp.where(base + before[e:e + 1] == slot_row, hits[e:e + 1], 0.0)
         token = jnp.sum(pick * token_lane + pick, axis=-1, keepdims=True) - 1.0
-        w = jnp.sum((taken * shares[e]).T[:slots], axis=-1, keepdims=True)
+        w = jnp.sum(pick * share, axis=-1, keepdims=True)
         high = w.astype(BF16).astype(F32)
         mid = (w - high).astype(BF16).astype(F32)
         low = w - high - mid
@@ -74,6 +69,16 @@
     for k in range(spread):
         peer = lax.rem(me + k, spread)
         outs[k][...] = rows_ref[lax.div(peer, GROUP)]
+
+
+def load_kernel(*refs):
+    half = (len(refs) - 1) // 2
+    sems = refs[-1]
+    copies = [pltpu.make_async_copy(refs[n], refs[half + n], sems.at[n]) for n in range(half)]
+    for copy in copies:
+        copy.start()
+    for copy in copies:
+        copy.wait()
 
 
 def feed_forward(h, wg_ref, wu_ref, wd_ref):
@@ -117,7 +122,7 @@
     gate = jnp.zeros((rows, wg_ref.shape[1]), F32)
     up = jnp.zeros((rows, wg_ref.shape[1]), F32)
     for s in range(sections):
-        h = (pieces[s] * scale * gain_ref[s:s + 1, :]).astype(BF16)
+        h = (pieces[s] * scale * gain_ref[:, s * feats:(s + 1) * feats]).astype(BF16)
         gate = gate + mm(h, wg_ref[s * feats:(s + 1) * feats, :])
         up = up + mm(h, wu_ref[s * feats:(s + 1) * feats, :])
     act = (gate / (1.0 + jnp.exp(-gate)) * up).astype(BF16)
@@ -145,7 +150,7 @@
     return x, send.astype(BF16)
 
 
-def table_kernel(x_ref, in_ref, x_out, send_out, cols_out, rows_out, *, sections, feats):
+def table_kernel(x_ref, in_ref, x_out, send_out, cols_out, rows_out, step_out, last_out, *, sections, feats):
     count, slots, padded = in_ref.shape
     tokens = x_ref.shape[0]
     total = count * slots
@@ -178,22 +183,25 @@
     cols = jnp.where(lane == 5, depth, cols)
     rows_tab = cols.T[:8]
     cols_out[...] = cols
+    step_out[0] = 1
+    last_out[0] = 2
     rows_out[...] = rows_tab
     x, send = apply_parts(0.0, parts, x_ref[...], cols, rows_tab, feats)
     x_out[...] = x
     send_out[...] = send.reshape(count, slots, padded)
 
 
-def update_kernel(step_ref, x_ref, in_ref, cols_ref, rows_ref, x_out, send_out, *, feats):
+def update_kernel(step_ref, x_ref, in_ref, cols_ref, rows_ref, x_out, send_out, step_out, *, feats):
     count, slots, padded = in_ref.shape
     step = step_ref[0].astype(F32)
+    step_out[0] = step_ref[0] + 1
     parts = in_ref[...].reshape(count * slots, padded)
     x, send = apply_parts(step, parts, x_ref[...], cols_ref[...], rows_ref[...], feats)
     x_out[...] = x
     send_out[...] = send.reshape(count, slots, padded)
 
 
-def call(kernel, out_shape, in_spaces, out_spaces, name, scratch=(), limit=None):
+def call(kernel, out_shape, in_spaces, out_spaces, name, scratch=(), limit=24 * 2**20, aliases={}):
     spec = lambda space: pl.BlockSpec(memory_space=space)
     single = not isinstance(out_shape, (list, tuple))
     return pl.pallas_call(
@@ -202,6 +210,7 @@
         in_specs=[spec(s) for s in in_spaces],
         out_specs=spec(out_spaces[0]) if single else [spec(s) for s in out_spaces],
         scratch_shapes=list(scratch),
+        input_output_aliases=aliases,
         compiler_params=pltpu.CompilerParams(vmem_limit_bytes=limit),
         name=name,
     )
@@ -219,21 +228,30 @@
     feats = width // sections
     padded = (feats // LANES + 1) * LANES
     devices = sections * spread
-    topk = route_ids.shape[-1]
-
-    wg, wu, wd = (w_gate[0], w_up[0], w_down[0])
+    by_token = lambda v: jnp.swapaxes(v[:, :, 0], 2, 3).reshape(ways * micro, v.shape[-1], tokens)
+
+    stored = [pltpu.with_memory_space_constraint(v[0], pltpu.HBM) for v in (w_gate, w_up, w_down)]
+    weights = call(
+        load_kernel,
+        [VMEM(v.shape, v.dtype) for v in stored],
+        [pltpu.HBM] * 3,
+        [VMEM] * 3,
+        "load",
+        scratch=[pltpu.SemaphoreType.DMA((3,))],
+    )(*stored)
+    wg, wu, wd = [pltpu.with_memory_space_constraint(v, VMEM) for v in weights]
     me = peer.astype(jnp.int32).reshape(1)
     flat = entering.reshape(everyone, width)
     sds = jax.ShapeDtypeStruct
 
     rows = call(
-        functools.partial(route_kernel, tokens=tokens, window=window, slots=slots),
+        functools.partial(route_kernel, window=window, slots=slots),
         [sds((slots, width + LANES), BF16)] * spread,
         [SMEM, VMEM, VMEM, VMEM],
         [VMEM] * spread,
         "route",
         scratch=[VMEM((window, slots, width + LANES), BF16)],
-    )(me, route_ids.reshape(everyone, topk), route_scores.reshape(everyone, topk), flat)
+    )(me, by_token(route_ids), by_token(route_scores), flat)
     received = [rows[0]] + [
         lax.ppermute(rows[k], "expert", [(y, (y + k) % spread) for y in range(spread)]) for k in range(1, spread)
     ]
@@ -248,38 +266,40 @@
     )(me, norm_gain, wg, wu, wd, *received)
     own = lax.dynamic_slice(flat, (0, section * feats), (everyone, feats))
     own = jnp.pad(own, ((0, 0), (0, padded - feats)))
-    x, send, cols, rows_tab = call(
+    parts, own = lax.optimization_barrier((parts, own))
+    number = sds((1,), jnp.int32)
+    state = sds((everyone, padded), BF16)
+    x, send, cols, rows_tab, step, last = call(
         functools.partial(table_kernel, sections=sections, feats=feats),
-        [sds((everyone, padded), BF16), message, sds((devices * slots, LANES), F32), sds((8, devices * slots), F32)],
+        [state, message, sds((devices * slots, LANES), F32), sds((8, devices * slots), F32), number, number],
         [VMEM, VMEM],
-        [VMEM] * 4,
+        [VMEM] * 4 + [SMEM] * 2,
         "table",
     )(own, swap(parts))
-    gain = norm_gain.reshape(sections, feats)
 
     def more(carry):
-        return carry[0] < carry[1]
+        return carry[0][0] < carry[1][0]
 
     def turn(carry):
-        step, unused, x, send = carry
+        step, unused, x, send = lax.optimization_barrier(carry)
         parts, last = call(
             functools.partial(round_kernel, sections=sections, feats=feats),
-            [message, sds((1,), jnp.int32)],
+            [message, number],
             [VMEM] * 5,
             [VMEM, SMEM],
             "round",
-        )(gain, wg, wu, wd, swap(send))
-        x, send = call(
+        )(norm_gain, wg, wu, wd, swap(send))
+        x, send, step = call(
             functools.partial(update_kernel, feats=feats),
-            [sds((everyone, padded), BF16), message],
+            [state, message, number],
             [SMEM] + [VMEM] * 4,
-            [VMEM] * 2,
+            [VMEM] * 2 + [SMEM],
             "update",
-        )(step.reshape(1), x, swap(parts), cols, rows_tab)
-        return (step + 1, last[0], x, send)
-
-    carry = (jnp.int32(1), jnp.int32(2), x, send)
-    x = lax.while_loop(more, turn, carry)[2]
+            aliases={1: 0},
+        )(step, x, swap(parts), cols, rows_tab)
+        return (step, last, x, send)
+
+    x = lax.while_loop(more, turn, (step, last, x, send))[2]
     return x[:, :feats].reshape(ways, micro, tokens, feats)
 
 

time: 149 us -> 127 us (0.85)
  blocking collectives: 38.9 us -> 91.9 us
  waiting for transfers between devices: 40.6 us -> 0.01 us
  Pallas kernels: 37.8 us -> 18 us
  starting transfers between devices: 18.3 us -> 4.52 us
  local copies, waits for them, and re-layouts: 10.6 us -> 4.3 us
  loops' own time: 2.04 us -> 7.08 us
    all_to_all x3 -> x7, blocking collectives: 38.9 us -> 91.9 us  [on_device(): lax.all_to_all(v, AXES, split_axis=0, concat_axis=0, tiled=True)]
    all_to_all x4 -> x0, waiting for transfers between devices: 38.5 us -> none  [on_device(): lax.all_to_all(v, AXES, split_axis=0, concat_axis=0, tiled=True)]
    all_to_all x4 -> x0, starting transfers between devices: 13.8 us -> none  [on_device(): lax.all_to_all(v, AXES, split_axis=0, concat_axis=0, tiled=True)]
    pallas_call x3, Pallas kernels: 21.5 us -> 8.12 us  [turn(): call(functools.partial(round_kernel, sections=sections, feats=feats), [me...]
    another operation x1, loops' own time: 2.04 us -> 7.08 us  [on_device(): x = lax.while_loop(more, turn, (step, last, x, send))[2]]
    pallas_call x1, Pallas kernels: 7.18 us -> 2.24 us  [on_device(): call(functools.partial(first_kernel, sections=sections, feats=feats), mes...]
    while x9 -> x0, local copies, waits for them, and re-layouts: 4.06 us -> none
    ppermute x3, waiting for transfers between devices: 2.16 us -> 0.01 us  [on_device(): lax.ppermute(rows[k], 'expert', [(y, (y + k) % spread) for y in range(spr...]
  transfers between devices with their start and end apart: 7 -> 3, of which waited for: 7 -> 0; matrix products, arithmetic and copies ran while one was open for 3% -> 1% of each run, Pallas kernels for 0% -> 3%
where the time goes in v2:
time: 127 us; the launch traced here: 126 us
  blocking collectives  91.9 us (72%)
  Pallas kernels  18 us (14%)
  loops' own time  7.08 us (6%)
  starting transfers between devices  4.52 us (4%)
  local copies, waits for them, and re-layouts  4.3 us (3%)
    all_to_all x7, blocking collectives, on_device(): lax.all_to_all(v, AXES, split_axis=0, concat_axis=0, tiled=True)  91.9 us
    pallas_call x3, Pallas kernels, turn(): call(functools.partial(round_kernel, sections=sections, feats=feats), [me...  8.12 us
    another operation x1, loops' own time, on_device(): x = lax.while_loop(more, turn, (step, last, x, send))[2]  7.08 us
    ppermute x3, starting transfers between devices, on_device(): lax.ppermute(rows[k], 'expert', [(y, (y + k) % spread) for y in range(spr...  4.52 us
    pallas_call x1, Pallas kernels, on_device(): call(load_kernel, [VMEM(v.shape, v.dtype) for v in stored], [pltpu.HBM] *...  4.23 us
    unnamed x10, local copies, waits for them, and re-layouts  3.27 us
  transfers between devices with their start and end apart: 3, of which 0 were waited for; matrix products, arithmetic and copies ran while one was open for 1% of the time, Pallas kernels for 3%

profile of v2, /device:TPU:0, one launch (start us, length us, event | category | flops | bytes accessed | tf_op | source)
XLA Modules:
  0.0 125.9 jit_solution(3710637533904470076)
XLA Ops:
  0.0 0.0 copy-start
  0.0 1.2 copy-done
  1.2 0.0 copy-start.1
  1.2 0.7 copy-done.1
  1.9 0.0 copy-start.2
  1.9 0.7 copy-done.2
  2.6 0.5 route.1
  3.2 0.5 collective-permute-start
  3.7 2.6 %collective-permute-start.1 = (bf16[8,3712]{1,0:T(8,128)(2,1)S(1)}, bf16[8,3712]{1,0:T(8,128)(2,1)S(1)}, u32[]{:S(2)}, u32[]{:S(2)}) collective-permute-start(bf16[8,3712]{1,0:T(8,128)(2,1)S(1)} %get-tuple-element.85), channel_id=1, source_target_pairs={{0,2},{1,3},{2,0},{3,1},{4,6},{5,7},{6,4},{7,5},{8,10},{9,11},{10,... | collective-permute-start | bytes 178184 | tf_op jit(solution)/shard_map/ppermute | solution.py:256
  6.3 1.4 %collective-permute-start.2 = (bf16[8,3712]{1,0:T(8,128)(2,1)S(1)}, bf16[8,3712]{1,0:T(8,128)(2,1)S(1)}, u32[]{:S(2)}, u32[]{:S(2)}) collective-permute-start(bf16[8,3712]{1,0:T(8,128)(2,1)S(1)} %get-tuple-element.86), channel_id=1, source_target_pairs={{0,3},{1,0},{2,1},{3,2},{4,7},{5,4},{6,5},{7,6},{8,11},{9,8},{10,9... | collective-permute-start | bytes 178184 | tf_op jit(solution)/shard_map/ppermute | solution.py:256
  7.7 1.0 constant_dynamic-slice_fusion
  8.7 0.0 copy-start.4
  8.7 4.2 %load.1 = (bf16[3584,512]{1,0:T(8,128)(2,1)S(1)}, bf16[3584,512]{1,0:T(8,128)(2,1)S(1)}, bf16[512,3584]{1,0:T(8,128)(2,1)S(1)}) custom-call(bf16[3584,512]{1,0:T(8,128)(2,1)} %bitcast.22, bf16[3584,512]{1,0:T(8,128)(2,1)} %bitcast.23, bf16[512,3584]{1,0:T(8,128)(2,1)} %bitcast.24), custom_call_target="tpu_custom_call" | custom-call | tf_op jit(solution)/shard_map/load/pallas_call | solution.py:234
  13.0 0.0 collective-permute-done.refs_1_
  13.0 0.0 collective-permute-done.1.refs_2_
  13.0 0.0 collective-permute-done.2.refs_3_
  13.0 0.0 copy-done.4
  13.0 2.2 %first.1 = bf16[32,8,512]{2,1,0:T(8,128)(2,1)S(1)} custom-call(s32[1]{0:T(128)} %bitcast.1.me_ref, f32[1,3584]{1,0:T(1,128)S(1)} %copy-done.4, bf16[3584,512]{1,0:T(8,128)(2,1)S(1)} %get-tuple-element.131.wg_ref, bf16[3584,512]{1,0:T(8,128)(2,1)S(1)} %get-tuple-element.132.wu_ref, bf16[512,3584]{1,0:T(8,128)(2,1)S(1)} %get-tuple-element.133.wd_ref, ...), custom_call_target="tpu_custom_call" | custom-call | tf_op jit(solution)/shard_map/first/pallas_call | solution.py:260
  15.3 15.3 %all_to_all.15.in_ref = bf16[32,8,512]{2,1,0:T(8,128)(2,1)S(1)} all-to-all(bf16[32,8,512]{2,1,0:T(8,128)(2,1)S(1)} %first.1), channel_id=1, replica_groups=mesh['section'=8,'expert'=4] {'section','expert'}, dimensions={0} | all-to-all | bytes 524288 | tf_op jit(solution)/shard_map/all_to_all | solution.py:259
  30.5 1.2 table.1
  31.8 93.5 %while.13 = (s32[1]{0:T(128)}, s32[1]{0:T(128)}, bf16[128,512]{1,0:T(8,128)(2,1)S(1)}, bf16[32,8,512]{2,1,0:T(8,128)(2,1)S(1)}, f32[1,3584]{1,0:T(1,128)S(1)}, /...) while((s32[1]{0:T(128)}, s32[1]{0:T(128)}, ...), condition=%region_1.2_spmd, body=%region_0.1_spmd | while | flops 1 | bytes 1048673 | solution.py:302
  33.0 12.8 %all_to_all.13.in_ref = bf16[32,8,512]{2,1,0:T(8,128)(2,1)S(1)} all-to-all(bf16[32,8,512]{2,1,0:T(8,128)(2,1)S(1)} %get-tuple-element.54), channel_id=1, replica_groups=mesh['section'=8,'expert'=4] {'section','expert'}, dimensions={0} | all-to-all | bytes 524288 | tf_op jit(solution)/shard_map/while/body/all_to_all | solution.py:259
  45.8 2.7 %round.1 = (bf16[32,8,512]{2,1,0:T(8,128)(2,1)S(1)}, s32[1]{0:T(128)}) custom-call(f32[1,3584]{1,0:T(1,128)S(1)} %get-tuple-element.150.gain_ref, bf16[3584,512]{1,0:T(8,128)(2,1)S(1)} %get-tuple-element.151.wg_ref, bf16[3584,512]{1,0:T(8,128)(2,1)S(1)} %get-tuple-element.152.wu_ref, bf16[512,3584]{1,0:T(8,128)(2,1)S(1)} %get-tuple-element.153.wd_ref, ...), custom_call_target="tpu_custom_call" | custom-call | tf_op jit(solution)/shard_map/while/body/round/pallas_call | solution.py:285
  48.5 12.8 %all_to_all.14.in_ref = bf16[32,8,512]{2,1,0:T(8,128)(2,1)S(1)} all-to-all(bf16[32,8,512]{2,1,0:T(8,128)(2,1)S(1)} %get-tuple-element.55), channel_id=1, replica_groups=mesh['section'=8,'expert'=4] {'section','expert'}, dimensions={0} | all-to-all | bytes 524288 | tf_op jit(solution)/shard_map/while/body/all_to_all | solution.py:259
  62.0 0.5 update.1
  63.8 12.8 %all_to_all.13.in_ref = bf16[32,8,512]{2,1,0:T(8,128)(2,1)S(1)} all-to-all(bf16[32,8,512]{2,1,0:T(8,128)(2,1)S(1)} %get-tuple-element.54), channel_id=1, replica_groups=mesh['section'=8,'expert'=4] {'section','expert'}, dimensions={0} | all-to-all | bytes 524288 | tf_op jit(solution)/shard_map/while/body/all_to_all | solution.py:259
  76.6 2.7 %round.1 = (bf16[32,8,512]{2,1,0:T(8,128)(2,1)S(1)}, s32[1]{0:T(128)}) custom-call(f32[1,3584]{1,0:T(1,128)S(1)} %get-tuple-element.150.gain_ref, bf16[3584,512]{1,0:T(8,128)(2,1)S(1)} %get-tuple-element.151.wg_ref, bf16[3584,512]{1,0:T(8,128)(2,1)S(1)} %get-tuple-element.152.wu_ref, bf16[512,3584]{1,0:T(8,128)(2,1)S(1)} %get-tuple-element.153.wd_ref, ...), custom_call_target="tpu_custom_call" | custom-call | tf_op jit(solution)/shard_map/while/body/round/pallas_call | solution.py:285
  79.3 12.8 %all_to_all.14.in_ref = bf16[32,8,512]{2,1,0:T(8,128)(2,1)S(1)} all-to-all(bf16[32,8,512]{2,1,0:T(8,128)(2,1)S(1)} %get-tuple-element.55), channel_id=1, replica_groups=mesh['section'=8,'expert'=4] {'section','expert'}, dimensions={0} | all-to-all | bytes 524288 | tf_op jit(solution)/shard_map/while/body/all_to_all | solution.py:259
  92.7 0.5 update.1
  94.5 12.8 %all_to_all.13.in_ref = bf16[32,8,512]{2,1,0:T(8,128)(2,1)S(1)} all-to-all(bf16[32,8,512]{2,1,0:T(8,128)(2,1)S(1)} %get-tuple-element.54), channel_id=1, replica_groups=mesh['section'=8,'expert'=4] {'section','expert'}, dimensions={0} | all-to-all | bytes 524288 | tf_op jit(solution)/shard_map/while/body/all_to_all | solution.py:259
  107.3 2.7 %round.1 = (bf16[32,8,512]{2,1,0:T(8,128)(2,1)S(1)}, s32[1]{0:T(128)}) custom-call(f32[1,3584]{1,0:T(1,128)S(1)} %get-tuple-element.150.gain_ref, bf16[3584,512]{1,0:T(8,128)(2,1)S(1)} %get-tuple-element.151.wg_ref, bf16[3584,512]{1,0:T(8,128)(2,1)S(1)} %get-tuple-element.152.wu_ref, bf16[512,3584]{1,0:T(8,128)(2,1)S(1)} %get-tuple-element.153.wd_ref, ...), custom_call_target="tpu_custom_call" | custom-call | tf_op jit(solution)/shard_map/while/body/round/pallas_call | solution.py:285
  110.0 12.8 %all_to_all.14.in_ref = bf16[32,8,512]{2,1,0:T(8,128)(2,1)S(1)} all-to-all(bf16[32,8,512]{2,1,0:T(8,128)(2,1)S(1)} %get-tuple-element.55), channel_id=1, replica_groups=mesh['section'=8,'expert'=4] {'section','expert'}, dimensions={0} | all-to-all | bytes 524288 | tf_op jit(solution)/shard_map/while/body/all_to_all | solution.py:259
  123.4 0.5 update.1
  125.3 0.0 copy-start.3
  125.3 0.6 copy-done.3
  (1 shorter events, 0.0 us)
Async XLA Ops:
  0.0 1.2 copy-start
  1.2 0.7 copy-start.1
  1.9 0.7 copy-start.2
  3.2 9.8 %collective-permute-start = (bf16[8,3712]{1,0:T(8,128)(2,1)S(1)}, bf16[8,3712]{1,0:T(8,128)(2,1)S(1)}, u32[]{:S(2)}, u32[]{:S(2)}) collective-permute-start(bf16[8,3712]{1,0:T(8,128)(2,1)S(1)} %get-tuple-element.84), channel_id=1, source_target_pairs={{0,1},{1,2},{2,3},{3,0},{4,5},{5,6},{6,7},{7,4},{8,9},{9,10},{10,1... | collective-permute-start | bytes 178184 | tf_op jit(solution)/shard_map/ppermute | solution.py:256
  3.7 9.3 %collective-permute-start.1 = (bf16[8,3712]{1,0:T(8,128)(2,1)S(1)}, bf16[8,3712]{1,0:T(8,128)(2,1)S(1)}, u32[]{:S(2)}, u32[]{:S(2)}) collective-permute-start(bf16[8,3712]{1,0:T(8,128)(2,1)S(1)} %get-tuple-element.85), channel_id=1, source_target_pairs={{0,2},{1,3},{2,0},{3,1},{4,6},{5,7},{6,4},{7,5},{8,10},{9,11},{10,... | collective-permute-start | bytes 178184 | tf_op jit(solution)/shard_map/ppermute | solution.py:256
  6.3 6.7 %collective-permute-start.2 = (bf16[8,3712]{1,0:T(8,128)(2,1)S(1)}, bf16[8,3712]{1,0:T(8,128)(2,1)S(1)}, u32[]{:S(2)}, u32[]{:S(2)}) collective-permute-start(bf16[8,3712]{1,0:T(8,128)(2,1)S(1)} %get-tuple-element.86), channel_id=1, source_target_pairs={{0,3},{1,0},{2,1},{3,2},{4,7},{5,4},{6,5},{7,6},{8,11},{9,8},{10,9... | collective-permute-start | bytes 178184 | tf_op jit(solution)/shard_map/ppermute | solution.py:256
  8.7 4.3 %copy-start.4 = (f32[1,3584]{1,0:T(1,128)S(1)}, f32[1,3584]{1,0:T(1,128)}, u32[]{:S(2)}) copy-start(f32[1,3584]{1,0:T(1,128)} %gain_ref.1) | copy-start | bytes 43012
  125.3 0.7 copy-start.3
